TPU v7x, 32 devices: a whole 2x2x4 slice. The times are simulated.
32 devices in a mesh: mesh: 16 (over z, x, core), band: 2 (over y).
Axes of the slice: x: 2, y: 2, z: 4, core: 2. Of those that a mesh axis runs over, the one named last changes fastest.
Arguments:
- band_block: bfloat16 [320, 4096], P('band', 'mesh'), may hold values from -6 to 6
- band_basis: bfloat16 [4096, 3072], P('mesh', 'band'), may hold values from -0.25 to 0.25
- mass_scale: float32 [4096], P('mesh'), may hold values from 0.7 to 1.5
- cell_matrices: bfloat16 [256, 4096], P('mesh')
- cell_nodes: int32 [256, 64], P('mesh'), may hold values from 0 to 319, as said below
- cell_count: int32 [16], P('mesh'), may hold values from 8 to 16, as said below
- send_index: int32 [16, 4, 16], P('mesh'), may hold values from 0 to 256, as said below
Outputs:
- filtered: bfloat16 [320, 4096], P('band', 'mesh')
- intersection: float32 [3072, 320], P('mesh', 'band')
- hamiltonian: float32 [3072, 320], P('mesh', 'band')
Inputs may be any that keep to these rules, and one draw needn't show every extreme that they name: `cell_nodes`: an entry below 256 is an owned node of the cell's partition; an entry 256 + k * 16 + c names ghost c of neighbour slot k, and c is always below the number of nodes that neighbour lists for this partition. In some partition the first cell's first entry is the last ghost slot, 319. send_index[p, k, :] lists, in ghost-slot order, owned nodes of partition p held by the partition (p + off(k)) mod 16; used slots come first and 256 marks an unused slot. Only partitions within 2 index steps (cyclically) share nodes. Some partition lists 16 nodes toward every neighbour and receives 16 from every neighbour. `cell_count`: some partition has all 16 cells live.
All inputs are finite; a program needn't handle non-finite values.
Results may differ from a plain program's by a relative error of at most 0.012.
Values may be sent and summed in bfloat16 or wider, within the bound.
A program may use at most 64 MiB of HBM per device.

v0:
```python
import jax
import jax.numpy as jnp
from jax import lax
from jax.sharding import PartitionSpec as P

filter_centre = 1.5
filter_half = 2.5
first_sigma = -0.625


def from_behind(value, axis, steps):
    count = lax.axis_size(axis)
    pairs = [(source, (source + steps) % count) for source in range(count)]
    return lax.ppermute(value, axis, pairs)


def sigma_values():
    values = [first_sigma]
    for _ in range(2):
        values.append(1.0 / (2.0 / first_sigma - values[-1]))
    return values


def neighbour_offset(neighbour, reach):
    if neighbour < reach:
        return neighbour + 1
    return reach - 1 - neighbour


def route_slots(outgoing, summing):
    width = outgoing.shape[1]
    reach = width // 2
    received = []
    for neighbour in range(width):
        partner = (neighbour + reach) % width
        moved_by = -neighbour_offset(neighbour, reach)
        if summing:
            received.append(from_behind(outgoing[:, partner], "mesh", moved_by))
        else:
            received.append(from_behind(outgoing[:, partner], "mesh", moved_by))
    return jnp.stack(received, axis=1)


def on_device(
    band_block, band_basis, mass_scale, cell_matrices, cell_nodes, cell_count, send_index
):
    columns = band_block.shape[0]
    owned_rows = band_block.shape[1]
    cell_slots = cell_nodes.shape[0]
    corners = cell_nodes.shape[1]
    send_rows = send_index[0]
    width = send_rows.shape[0]
    slot_count = send_rows.shape[1]
    live_mask = (jnp.arange(cell_slots, dtype=jnp.int32) < cell_count[0]).astype(jnp.float32)
    matrices = cell_matrices.reshape(cell_slots, corners, corners)
    flat_nodes = cell_nodes.reshape(-1)
    flat_sends = send_rows.reshape(-1)

    def operate(field):
        scaled = (mass_scale[None, :] * field.astype(jnp.float32)).astype(jnp.bfloat16)
        padded = jnp.concatenate([scaled, jnp.zeros((columns, 1), jnp.bfloat16)], axis=1)
        outgoing = padded[:, send_rows]
        ghosts = route_slots(outgoing, False)
        extended = jnp.concatenate([scaled, ghosts.reshape(columns, width * slot_count)], axis=1)
        gathered = extended[:, cell_nodes]
        products = jnp.einsum(
            "cij,bcj->bci", matrices, gathered, preferred_element_type=jnp.float32
        )
        products = products * live_mask[None, :, None]
        summed = jnp.zeros((columns, owned_rows + width * slot_count), jnp.float32)
        summed = summed.at[:, flat_nodes].add(products.reshape(columns, -1))
        returned = route_slots(summed[:, owned_rows:].reshape(columns, width, slot_count), True)
        owned_sum = jnp.concatenate(
            [summed[:, :owned_rows], jnp.zeros((columns, 1), jnp.float32)], axis=1
        )
        owned_sum = owned_sum.at[:, flat_sends].add(returned.reshape(columns, -1))[:, :owned_rows]
        return mass_scale[None, :] * owned_sum

    sigmas = sigma_values()
    previous = band_block
    applied = operate(band_block)
    current = (
        (applied - filter_centre * band_block.astype(jnp.float32)) * (sigmas[0] / filter_half)
    ).astype(jnp.bfloat16)
    for step in range(1, 3):
        applied = operate(current)
        scale_now = 2.0 * sigmas[step] / filter_half
        mixing = sigmas[step - 1] * sigmas[step]
        update = (
            applied - filter_centre * current.astype(jnp.float32)
        ) * scale_now - mixing * previous.astype(jnp.float32)
        previous = current
        current = update.astype(jnp.bfloat16)
    image = operate(current).astype(jnp.bfloat16)
    stacked = jnp.stack([current, image])
    tiles = jnp.einsum(
        "nr,skn->srk",
        lax.all_gather(band_basis, "band", axis=1, tiled=True),
        stacked,
        preferred_element_type=jnp.float32,
    )
    summed_tiles = lax.psum_scatter(tiles, "mesh", scatter_dimension=1, tiled=True)
    return (current, summed_tiles[0], summed_tiles[1])


def solution(mesh):
    placed = (
        P("band", "mesh"),
        P("mesh", "band"),
        P("mesh"),
        P("mesh", None),
        P("mesh", None),
        P("mesh"),
        P("mesh", None, None),
    )
    return jax.shard_map(
        on_device,
        mesh=mesh,
        in_specs=placed,
        out_specs=(P("band", "mesh"), P("mesh", "band"), P("mesh", "band")),
        check_vma=False,
    )
```

profile of v0, /device:TPU:0, one launch (start us, length us, event | category | flops | bytes accessed | tf_op | source)
XLA Modules:
  0.0 256.8 jit_solution(11110486246499141626)
XLA Ops:
  9.8 5.5 %collective-permute-start = (bf16[160,16]{0,1:T(8,128)(2,1)S(1)}, bf16[160,16]{0,1:T(8,128)(2,1)S(1)}, u32[]{:S(2)}, u32[]{:S(2)}) collective-permute-start(bf16[160,16]{0,1:T(8,128)(2,1)S(1)} %get-tuple-element.37), channel_id=1, source_target_pairs={{0,30},{2,0},{4,2},{6,4},{8,6},{10,8},{12,10},{14,12},{16,14},{18,... | collective-permute-start | bytes 15368 | tf_op jit(solution)/shard_map/ppermute | solution.py:14
  15.3 1.1 collective-permute-start.1
  20.3 1.2 reshape.152
  21.5 1.2 collective-permute-done.3
  23.0 3.9 %gather_fusion.1 = bf16[1024,160]{1,0:T(8,128)(2,1)S(1)} fusion(bf16[160,320]{0,1:T(8,128)(2,1)S(1)} %copy.56, s32[1024]{0:T(1024)S(1)} %broadcast_clamp_fusion), kind=kCustom, calls=%fused_computation.1 | custom fusion | bytes 659456 | tf_op jit(solution)/shard_map/gather | solution.py:65
  27.2 6.1 %scatter_custom_fusion = f32[160,320]{0,1:T(8,128)S(1)} fusion(s32[1024]{0:T(1024)S(1)} %bitcast.251, f32[1024,160]{1,0:T(8,128)S(1)} %bitcast.201, f32[]{:T(128)} %constant.13.clone.1), kind=kCustom, calls=%fused_computation.59 | custom fusion | flops 163840 | bytes 204804 | tf_op jit(solution)/shard_map/scatter-add | solution.py:71
  33.4 5.5 %collective-permute-start.4 = (f32[160,16]{0,1:T(8,128)S(1)}, f32[160,16]{0,1:T(8,128)S(1)}, u32[]{:S(2)}, u32[]{:S(2)}) collective-permute-start(f32[160,16]{0,1:T(8,128)S(1)} %get-tuple-element.21), channel_id=1, source_target_pairs={{0,30},{2,0},{4,2},{6,4},{8,6},{10,8},{12,10},{14,12},{16,14},{18,... | collective-permute-start | bytes 30728 | tf_op jit(solution)/shard_map/ppermute | solution.py:14
  38.9 4.7 %collective-permute-start.5 = (f32[160,16]{0,1:T(8,128)S(1)}, f32[160,16]{0,1:T(8,128)S(1)}, u32[]{:S(2)}, u32[]{:S(2)}) collective-permute-start(f32[160,16]{0,1:T(8,128)S(1)} %get-tuple-element.24), channel_id=1, source_target_pairs={{0,28},{2,30},{4,0},{6,2},{8,4},{10,6},{12,8},{14,10},{16,12},{18,... | collective-permute-start | bytes 30728 | tf_op jit(solution)/shard_map/ppermute | solution.py:14
  43.7 1.6 collective-permute-done.7
  47.4 3.3 %collective-permute-start.8 = (bf16[160,16]{0,1:T(8,128)(2,1)S(1)}, bf16[160,16]{0,1:T(8,128)(2,1)S(1)}, u32[]{:S(2)}, u32[]{:S(2)}) collective-permute-start(bf16[160,16]{0,1:T(8,128)(2,1)S(1)} %get-tuple-element.33), channel_id=1, source_target_pairs={{0,30},{2,0},{4,2},{6,4},{8,6},{10,8},{12,10},{14,12},{16,14},{18,... | collective-permute-start | bytes 15368 | tf_op jit(solution)/shard_map/ppermute | solution.py:14
  50.7 1.9 collective-permute-start.9
  52.8 3.7 %collective-permute-done.10 = bf16[160,16]{0,1:T(8,128)(2,1)S(1)} collective-permute-done((bf16[160,16]{0,1:T(8,128)(2,1)S(1)}, bf16[160,16]{0,1:T(8,128)(2,1)S(1)}, u32[]{:S(2)}, u32[]{:S(2)}) %collective-permute-start.10) | collective-permute-done | bytes 5152 | tf_op jit(solution)/shard_map/ppermute | solution.py:14
  56.5 2.5 collective-permute-done.11
  59.3 3.9 %gather_fusion.3 = bf16[1024,160]{1,0:T(8,128)(2,1)S(1)} fusion(bf16[160,320]{0,1:T(8,128)(2,1)S(1)} %copy.60, s32[1024]{0:T(1024)S(1)} %broadcast_clamp_fusion), kind=kCustom, calls=%fused_computation.3 | custom fusion | bytes 659456 | tf_op jit(solution)/shard_map/gather | solution.py:65
  63.5 6.1 %scatter_custom_fusion.2 = f32[160,320]{0,1:T(8,128)S(1)} fusion(s32[1024]{0:T(1024)S(1)} %bitcast.252, f32[1024,160]{1,0:T(8,128)S(1)} %bitcast.202, f32[]{:T(128)} %constant.13.clone.1), kind=kCustom, calls=%fused_computation.57 | custom fusion | flops 163840 | bytes 204804 | tf_op jit(solution)/shard_map/scatter-add | solution.py:71
  69.7 1.4 collective-permute-start.12
  71.1 1.7 collective-permute-start.15
  72.9 3.0 %collective-permute-start.13 = (f32[160,16]{0,1:T(8,128)S(1)}, f32[160,16]{0,1:T(8,128)S(1)}, u32[]{:S(2)}, u32[]{:S(2)}) collective-permute-start(f32[160,16]{0,1:T(8,128)S(1)} %get-tuple-element.20), channel_id=1, source_target_pairs={{0,28},{2,30},{4,0},{6,2},{8,4},{10,6},{12,8},{14,10},{16,12},{18,... | collective-permute-start | bytes 30728 | tf_op jit(solution)/shard_map/ppermute | solution.py:14
  76.0 1.6 collective-permute-done.15
  77.6 1.2 collective-permute-done.14
  80.8 3.9 %collective-permute-start.16 = (bf16[160,16]{0,1:T(8,128)(2,1)S(1)}, bf16[160,16]{0,1:T(8,128)(2,1)S(1)}, u32[]{:S(2)}, u32[]{:S(2)}) collective-permute-start(bf16[160,16]{0,1:T(8,128)(2,1)S(1)} %get-tuple-element.29), channel_id=1, source_target_pairs={{0,30},{2,0},{4,2},{6,4},{8,6},{10,8},{12,10},{14,12},{16,14},{18,... | collective-permute-start | bytes 15368 | tf_op jit(solution)/shard_map/ppermute | solution.py:14
  85.2 1.6 collective-permute-start.19
  87.0 3.5 %collective-permute-done.18 = bf16[160,16]{0,1:T(8,128)(2,1)S(1)} collective-permute-done((bf16[160,16]{0,1:T(8,128)(2,1)S(1)}, bf16[160,16]{0,1:T(8,128)(2,1)S(1)}, u32[]{:S(2)}, u32[]{:S(2)}) %collective-permute-start.18) | collective-permute-done | bytes 5152 | tf_op jit(solution)/shard_map/ppermute | solution.py:14
  90.5 1.0 collective-permute-done.19
  91.8 3.9 %gather_fusion.5 = bf16[1024,160]{1,0:T(8,128)(2,1)S(1)} fusion(bf16[160,320]{0,1:T(8,128)(2,1)S(1)} %copy.64, s32[1024]{0:T(1024)S(1)} %broadcast_clamp_fusion), kind=kCustom, calls=%fused_computation.5 | custom fusion | bytes 659456 | tf_op jit(solution)/shard_map/gather | solution.py:65
  96.1 6.1 %scatter_custom_fusion.4 = f32[160,320]{0,1:T(8,128)S(1)} fusion(s32[1024]{0:T(1024)S(1)} %bitcast.253, f32[1024,160]{1,0:T(8,128)S(1)} %bitcast.203, f32[]{:T(128)} %constant.13.clone.1), kind=kCustom, calls=%fused_computation.55 | custom fusion | flops 163840 | bytes 204804 | tf_op jit(solution)/shard_map/scatter-add | solution.py:71
  102.2 2.9 %collective-permute-start.20 = (f32[160,16]{0,1:T(8,128)S(1)}, f32[160,16]{0,1:T(8,128)S(1)}, u32[]{:S(2)}, u32[]{:S(2)}) collective-permute-start(f32[160,16]{0,1:T(8,128)S(1)} %get-tuple-element.13), channel_id=1, source_target_pairs={{0,30},{2,0},{4,2},{6,4},{8,6},{10,8},{12,10},{14,12},{16,14},{18,... | collective-permute-start | bytes 30728 | tf_op jit(solution)/shard_map/ppermute | solution.py:14
  105.1 1.7 collective-permute-start.23
  106.9 3.0 %collective-permute-start.21 = (f32[160,16]{0,1:T(8,128)S(1)}, f32[160,16]{0,1:T(8,128)S(1)}, u32[]{:S(2)}, u32[]{:S(2)}) collective-permute-start(f32[160,16]{0,1:T(8,128)S(1)} %get-tuple-element.16), channel_id=1, source_target_pairs={{0,28},{2,30},{4,0},{6,2},{8,4},{10,6},{12,8},{14,10},{16,12},{18,... | collective-permute-start | bytes 30728 | tf_op jit(solution)/shard_map/ppermute | solution.py:14
  110.0 1.6 collective-permute-done.23
  111.5 1.2 collective-permute-done.22
  114.9 3.9 %collective-permute-start.24 = (bf16[160,16]{0,1:T(8,128)(2,1)S(1)}, bf16[160,16]{0,1:T(8,128)(2,1)S(1)}, u32[]{:S(2)}, u32[]{:S(2)}) collective-permute-start(bf16[160,16]{0,1:T(8,128)(2,1)S(1)} %get-tuple-element.25), channel_id=1, source_target_pairs={{0,30},{2,0},{4,2},{6,4},{8,6},{10,8},{12,10},{14,12},{16,14},{18,... | collective-permute-start | bytes 15368 | tf_op jit(solution)/shard_map/ppermute | solution.py:14
  119.2 1.6 collective-permute-start.27
  120.8 3.7 %collective-permute-done.26 = bf16[160,16]{0,1:T(8,128)(2,1)S(1)} collective-permute-done((bf16[160,16]{0,1:T(8,128)(2,1)S(1)}, bf16[160,16]{0,1:T(8,128)(2,1)S(1)}, u32[]{:S(2)}, u32[]{:S(2)}) %collective-permute-start.26) | collective-permute-done | bytes 5152 | tf_op jit(solution)/shard_map/ppermute | solution.py:14
  124.5 1.0 collective-permute-done.27
  125.9 3.9 %gather_fusion.7 = bf16[1024,160]{1,0:T(8,128)(2,1)S(1)} fusion(bf16[160,320]{0,1:T(8,128)(2,1)S(1)} %copy.68, s32[1024]{0:T(1024)S(1)} %broadcast_clamp_fusion), kind=kCustom, calls=%fused_computation.7 | custom fusion | bytes 659456 | tf_op jit(solution)/shard_map/gather | solution.py:65
  130.1 6.1 %scatter_custom_fusion.6 = f32[160,320]{0,1:T(8,128)S(1)} fusion(s32[1024]{0:T(1024)S(1)} %bitcast.254, f32[1024,160]{1,0:T(8,128)S(1)} %bitcast.200, f32[]{:T(128)} %constant.13.clone.1), kind=kCustom, calls=%fused_computation.53 | custom fusion | flops 163840 | bytes 204804 | tf_op jit(solution)/shard_map/scatter-add | solution.py:71
  136.3 2.9 %collective-permute-start.28 = (f32[160,16]{0,1:T(8,128)S(1)}, f32[160,16]{0,1:T(8,128)S(1)}, u32[]{:S(2)}, u32[]{:S(2)}) collective-permute-start(f32[160,16]{0,1:T(8,128)S(1)} %get-tuple-element.9), channel_id=1, source_target_pairs={{0,30},{2,0},{4,2},{6,4},{8,6},{10,8},{12,10},{14,12},{16,14},{18,... | collective-permute-start | bytes 30728 | tf_op jit(solution)/shard_map/ppermute | solution.py:14
  139.2 1.7 collective-permute-start.31
  140.9 3.0 %collective-permute-start.29 = (f32[160,16]{0,1:T(8,128)S(1)}, f32[160,16]{0,1:T(8,128)S(1)}, u32[]{:S(2)}, u32[]{:S(2)}) collective-permute-start(f32[160,16]{0,1:T(8,128)S(1)} %get-tuple-element.12), channel_id=1, source_target_pairs={{0,28},{2,30},{4,0},{6,2},{8,4},{10,6},{12,8},{14,10},{16,12},{18,... | collective-permute-start | bytes 30728 | tf_op jit(solution)/shard_map/ppermute | solution.py:14
  144.0 1.6 collective-permute-done.31
  145.6 1.2 collective-permute-done.30
  146.8 1.2 scatter_fusion.3
  148.2 4.0 %convolution_bitcast_fusion = f32[2,3072,160]{1,2,0:T(8,128)} fusion(bf16[256,3072]{1,0:T(8,128)(2,1)} %all-gather.2.cloned.1.call-done, bf16[1,160,256]{2,1,0:T(8,128)(2,1)S(1)} %fusion.26, bf16[1,160,256]{2,1,0:T(8,128)(2,1)S(1)} %bitcast.208), kind=kOutput, calls=%fused_computation.16 | convolution fusion | flops 503398400 | bytes 5668864 | tf_op jit(solution)/shard_map/nr,skn->srk/dot_general | solution.py:96
  152.2 9.6 %copy.70 = f32[2,3072,160]{2,0,1:T(2,128)} copy(f32[2,3072,160]{1,2,0:T(8,128)} %convolution_bitcast_fusion) | data formatting | bytes 7864320
  161.8 8.6 %reshape.309 = f32[3072,320]{1,0:T(8,128)} reshape(f32[3072,2,160]{2,1,0:T(2,128)} %bitcast.190) | data formatting | bytes 7864320
  170.5 76.4 %reduce-scatter.4.cloned.1.call-done = f32[192,320]{1,0:T(8,128)} async-done(((f32[3072,320]{1,0:T(8,128)}), f32[192,320]{1,0:T(8,128)}) %reduce-scatter.4.cloned.1.call-update) | async-done | bytes 245776
  246.8 1.3 reshape.310
  (126 shorter events, 18.0 us)
Async XLA Ops:
  7.2 141.0 %all-gather.2.cloned.1.call-start = ((), (), s32[]{:S(2)}) async-start(), calls=%async_computation.1 | async-start | bytes 2359296 | tf_op jit(solution)/shard_map/all_gather | solution.py:98
  9.8 11.7 %collective-permute-start = (bf16[160,16]{0,1:T(8,128)(2,1)S(1)}, bf16[160,16]{0,1:T(8,128)(2,1)S(1)}, u32[]{:S(2)}, u32[]{:S(2)}) collective-permute-start(bf16[160,16]{0,1:T(8,128)(2,1)S(1)} %get-tuple-element.37), channel_id=1, source_target_pairs={{0,30},{2,0},{4,2},{6,4},{8,6},{10,8},{12,10},{14,12},{16,14},{18,... | collective-permute-start | bytes 15368 | tf_op jit(solution)/shard_map/ppermute | solution.py:14
  15.2 6.2 %collective-permute-start.2 = (bf16[160,16]{0,1:T(8,128)(2,1)S(1)}, bf16[160,16]{0,1:T(8,128)(2,1)S(1)}, u32[]{:S(2)}, u32[]{:S(2)}) collective-permute-start(bf16[160,16]{0,1:T(8,128)(2,1)S(1)} %get-tuple-element.38), channel_id=1, source_target_pairs={{0,2},{2,4},{4,6},{6,8},{8,10},{10,12},{12,14},{14,16},{16,18},{18... | collective-permute-start | bytes 15368 | tf_op jit(solution)/shard_map/ppermute | solution.py:14
  15.3 6.2 %collective-permute-start.1 = (bf16[160,16]{0,1:T(8,128)(2,1)S(1)}, bf16[160,16]{0,1:T(8,128)(2,1)S(1)}, u32[]{:S(2)}, u32[]{:S(2)}) collective-permute-start(bf16[160,16]{0,1:T(8,128)(2,1)S(1)} %get-tuple-element.39), channel_id=1, source_target_pairs={{0,28},{2,30},{4,0},{6,2},{8,4},{10,6},{12,8},{14,10},{16,12},{18,... | collective-permute-start | bytes 15368 | tf_op jit(solution)/shard_map/ppermute | solution.py:14
  16.3 6.3 %collective-permute-start.3 = (bf16[160,16]{0,1:T(8,128)(2,1)S(1)}, bf16[160,16]{0,1:T(8,128)(2,1)S(1)}, u32[]{:S(2)}, u32[]{:S(2)}) collective-permute-start(bf16[160,16]{0,1:T(8,128)(2,1)S(1)} %get-tuple-element.40), channel_id=1, source_target_pairs={{0,4},{2,6},{4,8},{6,10},{8,12},{10,14},{12,16},{14,18},{16,20},{1... | collective-permute-start | bytes 15368 | tf_op jit(solution)/shard_map/ppermute | solution.py:14
  23.0 20.6 %copy-start.3 = (pred[257]{0:T(512)(128)(4,1)S(1)}, pred[257]{0:T(512)(128)(4,1)}, u32[]{:S(2)}) copy-start(pred[257]{0:T(512)(128)(4,1)} %constant.12.clone.1) | copy-start | bytes 775
  26.9 19.6 %copy-start = (bf16[160,256]{1,0:T(8,128)(2,1)S(1)}, bf16[160,256]{1,0:T(8,128)(2,1)}, u32[]{:S(2)}) copy-start(bf16[160,256]{1,0:T(8,128)(2,1)} %param.7) | copy-start | bytes 245764
  26.9 19.6 %copy-start.2 = (f32[256]{0:T(256)S(1)}, f32[256]{0:T(256)}, u32[]{:S(2)}) copy-start(f32[256]{0:T(256)} %param.9) | copy-start | bytes 3076
  33.4 10.3 %collective-permute-start.4 = (f32[160,16]{0,1:T(8,128)S(1)}, f32[160,16]{0,1:T(8,128)S(1)}, u32[]{:S(2)}, u32[]{:S(2)}) collective-permute-start(f32[160,16]{0,1:T(8,128)S(1)} %get-tuple-element.21), channel_id=1, source_target_pairs={{0,30},{2,0},{4,2},{6,4},{8,6},{10,8},{12,10},{14,12},{16,14},{18,... | collective-permute-start | bytes 30728 | tf_op jit(solution)/shard_map/ppermute | solution.py:14
  38.9 6.4 %collective-permute-start.7 = (f32[160,16]{0,1:T(8,128)S(1)}, f32[160,16]{0,1:T(8,128)S(1)}, u32[]{:S(2)}, u32[]{:S(2)}) collective-permute-start(f32[160,16]{0,1:T(8,128)S(1)} %get-tuple-element.22), channel_id=1, source_target_pairs={{0,4},{2,6},{4,8},{6,10},{8,12},{10,14},{12,16},{14,18},{16,20},{1... | collective-permute-start | bytes 30728 | tf_op jit(solution)/shard_map/ppermute | solution.py:14
  38.9 6.4 %collective-permute-start.6 = (f32[160,16]{0,1:T(8,128)S(1)}, f32[160,16]{0,1:T(8,128)S(1)}, u32[]{:S(2)}, u32[]{:S(2)}) collective-permute-start(f32[160,16]{0,1:T(8,128)S(1)} %get-tuple-element.23), channel_id=1, source_target_pairs={{0,2},{2,4},{4,6},{6,8},{8,10},{10,12},{12,14},{14,16},{16,18},{18... | collective-permute-start | bytes 30728 | tf_op jit(solution)/shard_map/ppermute | solution.py:14
  38.9 6.4 %collective-permute-start.5 = (f32[160,16]{0,1:T(8,128)S(1)}, f32[160,16]{0,1:T(8,128)S(1)}, u32[]{:S(2)}, u32[]{:S(2)}) collective-permute-start(f32[160,16]{0,1:T(8,128)S(1)} %get-tuple-element.24), channel_id=1, source_target_pairs={{0,28},{2,30},{4,0},{6,2},{8,4},{10,6},{12,8},{14,10},{16,12},{18,... | collective-permute-start | bytes 30728 | tf_op jit(solution)/shard_map/ppermute | solution.py:14
  47.4 5.4 %collective-permute-start.8 = (bf16[160,16]{0,1:T(8,128)(2,1)S(1)}, bf16[160,16]{0,1:T(8,128)(2,1)S(1)}, u32[]{:S(2)}, u32[]{:S(2)}) collective-permute-start(bf16[160,16]{0,1:T(8,128)(2,1)S(1)} %get-tuple-element.33), channel_id=1, source_target_pairs={{0,30},{2,0},{4,2},{6,4},{8,6},{10,8},{12,10},{14,12},{16,14},{18,... | collective-permute-start | bytes 15368 | tf_op jit(solution)/shard_map/ppermute | solution.py:14
  50.7 5.8 %collective-permute-start.10 = (bf16[160,16]{0,1:T(8,128)(2,1)S(1)}, bf16[160,16]{0,1:T(8,128)(2,1)S(1)}, u32[]{:S(2)}, u32[]{:S(2)}) collective-permute-start(bf16[160,16]{0,1:T(8,128)(2,1)S(1)} %get-tuple-element.34), channel_id=1, source_target_pairs={{0,2},{2,4},{4,6},{6,8},{8,10},{10,12},{12,14},{14,16},{16,18},{18... | collective-permute-start | bytes 15368 | tf_op jit(solution)/shard_map/ppermute | solution.py:14
  50.7 5.8 %collective-permute-start.9 = (bf16[160,16]{0,1:T(8,128)(2,1)S(1)}, bf16[160,16]{0,1:T(8,128)(2,1)S(1)}, u32[]{:S(2)}, u32[]{:S(2)}) collective-permute-start(bf16[160,16]{0,1:T(8,128)(2,1)S(1)} %get-tuple-element.35), channel_id=1, source_target_pairs={{0,28},{2,30},{4,0},{6,2},{8,4},{10,6},{12,8},{14,10},{16,12},{18,... | collective-permute-start | bytes 15368 | tf_op jit(solution)/shard_map/ppermute | solution.py:14
  52.7 6.3 %collective-permute-start.11 = (bf16[160,16]{0,1:T(8,128)(2,1)S(1)}, bf16[160,16]{0,1:T(8,128)(2,1)S(1)}, u32[]{:S(2)}, u32[]{:S(2)}) collective-permute-start(bf16[160,16]{0,1:T(8,128)(2,1)S(1)} %get-tuple-element.36), channel_id=1, source_target_pairs={{0,4},{2,6},{4,8},{6,10},{8,12},{10,14},{12,16},{14,18},{16,20},{1... | collective-permute-start | bytes 15368 | tf_op jit(solution)/shard_map/ppermute | solution.py:14
  69.7 6.2 %collective-permute-start.12 = (f32[160,16]{0,1:T(8,128)S(1)}, f32[160,16]{0,1:T(8,128)S(1)}, u32[]{:S(2)}, u32[]{:S(2)}) collective-permute-start(f32[160,16]{0,1:T(8,128)S(1)} %get-tuple-element.17), channel_id=1, source_target_pairs={{0,30},{2,0},{4,2},{6,4},{8,6},{10,8},{12,10},{14,12},{16,14},{18,... | collective-permute-start | bytes 30728 | tf_op jit(solution)/shard_map/ppermute | solution.py:14
  71.1 6.4 %collective-permute-start.15 = (f32[160,16]{0,1:T(8,128)S(1)}, f32[160,16]{0,1:T(8,128)S(1)}, u32[]{:S(2)}, u32[]{:S(2)}) collective-permute-start(f32[160,16]{0,1:T(8,128)S(1)} %get-tuple-element.18), channel_id=1, source_target_pairs={{0,4},{2,6},{4,8},{6,10},{8,12},{10,14},{12,16},{14,18},{16,20},{1... | collective-permute-start | bytes 30728 | tf_op jit(solution)/shard_map/ppermute | solution.py:14
  72.9 5.9 %collective-permute-start.14 = (f32[160,16]{0,1:T(8,128)S(1)}, f32[160,16]{0,1:T(8,128)S(1)}, u32[]{:S(2)}, u32[]{:S(2)}) collective-permute-start(f32[160,16]{0,1:T(8,128)S(1)} %get-tuple-element.19), channel_id=1, source_target_pairs={{0,2},{2,4},{4,6},{6,8},{8,10},{10,12},{12,14},{14,16},{16,18},{18... | collective-permute-start | bytes 30728 | tf_op jit(solution)/shard_map/ppermute | solution.py:14
  72.9 5.9 %collective-permute-start.13 = (f32[160,16]{0,1:T(8,128)S(1)}, f32[160,16]{0,1:T(8,128)S(1)}, u32[]{:S(2)}, u32[]{:S(2)}) collective-permute-start(f32[160,16]{0,1:T(8,128)S(1)} %get-tuple-element.20), channel_id=1, source_target_pairs={{0,28},{2,30},{4,0},{6,2},{8,4},{10,6},{12,8},{14,10},{16,12},{18,... | collective-permute-start | bytes 30728 | tf_op jit(solution)/shard_map/ppermute | solution.py:14
  80.8 6.2 %collective-permute-start.16 = (bf16[160,16]{0,1:T(8,128)(2,1)S(1)}, bf16[160,16]{0,1:T(8,128)(2,1)S(1)}, u32[]{:S(2)}, u32[]{:S(2)}) collective-permute-start(bf16[160,16]{0,1:T(8,128)(2,1)S(1)} %get-tuple-element.29), channel_id=1, source_target_pairs={{0,30},{2,0},{4,2},{6,4},{8,6},{10,8},{12,10},{14,12},{16,14},{18,... | collective-permute-start | bytes 15368 | tf_op jit(solution)/shard_map/ppermute | solution.py:14
  84.7 5.8 %collective-permute-start.18 = (bf16[160,16]{0,1:T(8,128)(2,1)S(1)}, bf16[160,16]{0,1:T(8,128)(2,1)S(1)}, u32[]{:S(2)}, u32[]{:S(2)}) collective-permute-start(bf16[160,16]{0,1:T(8,128)(2,1)S(1)} %get-tuple-element.30), channel_id=1, source_target_pairs={{0,2},{2,4},{4,6},{6,8},{8,10},{10,12},{12,14},{14,16},{16,18},{18... | collective-permute-start | bytes 15368 | tf_op jit(solution)/shard_map/ppermute | solution.py:14
  84.7 5.8 %collective-permute-start.17 = (bf16[160,16]{0,1:T(8,128)(2,1)S(1)}, bf16[160,16]{0,1:T(8,128)(2,1)S(1)}, u32[]{:S(2)}, u32[]{:S(2)}) collective-permute-start(bf16[160,16]{0,1:T(8,128)(2,1)S(1)} %get-tuple-element.31), channel_id=1, source_target_pairs={{0,28},{2,30},{4,0},{6,2},{8,4},{10,6},{12,8},{14,10},{16,12},{18,... | collective-permute-start | bytes 15368 | tf_op jit(solution)/shard_map/ppermute | solution.py:14
  85.2 6.3 %collective-permute-start.19 = (bf16[160,16]{0,1:T(8,128)(2,1)S(1)}, bf16[160,16]{0,1:T(8,128)(2,1)S(1)}, u32[]{:S(2)}, u32[]{:S(2)}) collective-permute-start(bf16[160,16]{0,1:T(8,128)(2,1)S(1)} %get-tuple-element.32), channel_id=1, source_target_pairs={{0,4},{2,6},{4,8},{6,10},{8,12},{10,14},{12,16},{14,18},{16,20},{1... | collective-permute-start | bytes 15368 | tf_op jit(solution)/shard_map/ppermute | solution.py:14
  86.8 160.0 %reduce-scatter.4.cloned.1.call-start = ((), (), s32[]{:S(2)}) async-start(), calls=%async_computation.2 | async-start | bytes 5013504
  102.2 7.7 %collective-permute-start.20 = (f32[160,16]{0,1:T(8,128)S(1)}, f32[160,16]{0,1:T(8,128)S(1)}, u32[]{:S(2)}, u32[]{:S(2)}) collective-permute-start(f32[160,16]{0,1:T(8,128)S(1)} %get-tuple-element.13), channel_id=1, source_target_pairs={{0,30},{2,0},{4,2},{6,4},{8,6},{10,8},{12,10},{14,12},{16,14},{18,... | collective-permute-start | bytes 30728 | tf_op jit(solution)/shard_map/ppermute | solution.py:14
  105.1 6.4 %collective-permute-start.23 = (f32[160,16]{0,1:T(8,128)S(1)}, f32[160,16]{0,1:T(8,128)S(1)}, u32[]{:S(2)}, u32[]{:S(2)}) collective-permute-start(f32[160,16]{0,1:T(8,128)S(1)} %get-tuple-element.14), channel_id=1, source_target_pairs={{0,4},{2,6},{4,8},{6,10},{8,12},{10,14},{12,16},{14,18},{16,20},{1... | collective-permute-start | bytes 30728 | tf_op jit(solution)/shard_map/ppermute | solution.py:14
  106.9 5.9 %collective-permute-start.22 = (f32[160,16]{0,1:T(8,128)S(1)}, f32[160,16]{0,1:T(8,128)S(1)}, u32[]{:S(2)}, u32[]{:S(2)}) collective-permute-start(f32[160,16]{0,1:T(8,128)S(1)} %get-tuple-element.15), channel_id=1, source_target_pairs={{0,2},{2,4},{4,6},{6,8},{8,10},{10,12},{12,14},{14,16},{16,18},{18... | collective-permute-start | bytes 30728 | tf_op jit(solution)/shard_map/ppermute | solution.py:14
  106.9 5.9 %collective-permute-start.21 = (f32[160,16]{0,1:T(8,128)S(1)}, f32[160,16]{0,1:T(8,128)S(1)}, u32[]{:S(2)}, u32[]{:S(2)}) collective-permute-start(f32[160,16]{0,1:T(8,128)S(1)} %get-tuple-element.16), channel_id=1, source_target_pairs={{0,28},{2,30},{4,0},{6,2},{8,4},{10,6},{12,8},{14,10},{16,12},{18,... | collective-permute-start | bytes 30728 | tf_op jit(solution)/shard_map/ppermute | solution.py:14
  114.0 34.2 %copy-start.1 = (bf16[160,256]{1,0:T(8,128)(2,1)}, bf16[160,256]{1,0:T(8,128)(2,1)S(1)}, u32[]{:S(2)}) copy-start(bf16[160,256]{1,0:T(8,128)(2,1)S(1)} %get-tuple-element.4) | copy-start | bytes 245764
  114.9 5.9 %collective-permute-start.24 = (bf16[160,16]{0,1:T(8,128)(2,1)S(1)}, bf16[160,16]{0,1:T(8,128)(2,1)S(1)}, u32[]{:S(2)}, u32[]{:S(2)}) collective-permute-start(bf16[160,16]{0,1:T(8,128)(2,1)S(1)} %get-tuple-element.25), channel_id=1, source_target_pairs={{0,30},{2,0},{4,2},{6,4},{8,6},{10,8},{12,10},{14,12},{16,14},{18,... | collective-permute-start | bytes 15368 | tf_op jit(solution)/shard_map/ppermute | solution.py:14
  118.8 5.8 %collective-permute-start.26 = (bf16[160,16]{0,1:T(8,128)(2,1)S(1)}, bf16[160,16]{0,1:T(8,128)(2,1)S(1)}, u32[]{:S(2)}, u32[]{:S(2)}) collective-permute-start(bf16[160,16]{0,1:T(8,128)(2,1)S(1)} %get-tuple-element.26), channel_id=1, source_target_pairs={{0,2},{2,4},{4,6},{6,8},{8,10},{10,12},{12,14},{14,16},{16,18},{18... | collective-permute-start | bytes 15368 | tf_op jit(solution)/shard_map/ppermute | solution.py:14
  118.8 5.8 %collective-permute-start.25 = (bf16[160,16]{0,1:T(8,128)(2,1)S(1)}, bf16[160,16]{0,1:T(8,128)(2,1)S(1)}, u32[]{:S(2)}, u32[]{:S(2)}) collective-permute-start(bf16[160,16]{0,1:T(8,128)(2,1)S(1)} %get-tuple-element.27), channel_id=1, source_target_pairs={{0,28},{2,30},{4,0},{6,2},{8,4},{10,6},{12,8},{14,10},{16,12},{18,... | collective-permute-start | bytes 15368 | tf_op jit(solution)/shard_map/ppermute | solution.py:14
  119.2 6.3 %collective-permute-start.27 = (bf16[160,16]{0,1:T(8,128)(2,1)S(1)}, bf16[160,16]{0,1:T(8,128)(2,1)S(1)}, u32[]{:S(2)}, u32[]{:S(2)}) collective-permute-start(bf16[160,16]{0,1:T(8,128)(2,1)S(1)} %get-tuple-element.28), channel_id=1, source_target_pairs={{0,4},{2,6},{4,8},{6,10},{8,12},{10,14},{12,16},{14,18},{16,20},{1... | collective-permute-start | bytes 15368 | tf_op jit(solution)/shard_map/ppermute | solution.py:14
  136.3 7.7 %collective-permute-start.28 = (f32[160,16]{0,1:T(8,128)S(1)}, f32[160,16]{0,1:T(8,128)S(1)}, u32[]{:S(2)}, u32[]{:S(2)}) collective-permute-start(f32[160,16]{0,1:T(8,128)S(1)} %get-tuple-element.9), channel_id=1, source_target_pairs={{0,30},{2,0},{4,2},{6,4},{8,6},{10,8},{12,10},{14,12},{16,14},{18,... | collective-permute-start | bytes 30728 | tf_op jit(solution)/shard_map/ppermute | solution.py:14
  139.2 6.4 %collective-permute-start.31 = (f32[160,16]{0,1:T(8,128)S(1)}, f32[160,16]{0,1:T(8,128)S(1)}, u32[]{:S(2)}, u32[]{:S(2)}) collective-permute-start(f32[160,16]{0,1:T(8,128)S(1)} %get-tuple-element.10), channel_id=1, source_target_pairs={{0,4},{2,6},{4,8},{6,10},{8,12},{10,14},{12,16},{14,18},{16,20},{1... | collective-permute-start | bytes 30728 | tf_op jit(solution)/shard_map/ppermute | solution.py:14
  140.9 5.9 %collective-permute-start.30 = (f32[160,16]{0,1:T(8,128)S(1)}, f32[160,16]{0,1:T(8,128)S(1)}, u32[]{:S(2)}, u32[]{:S(2)}) collective-permute-start(f32[160,16]{0,1:T(8,128)S(1)} %get-tuple-element.11), channel_id=1, source_target_pairs={{0,2},{2,4},{4,6},{6,8},{8,10},{10,12},{12,14},{14,16},{16,18},{18... | collective-permute-start | bytes 30728 | tf_op jit(solution)/shard_map/ppermute | solution.py:14
  140.9 5.9 %collective-permute-start.29 = (f32[160,16]{0,1:T(8,128)S(1)}, f32[160,16]{0,1:T(8,128)S(1)}, u32[]{:S(2)}, u32[]{:S(2)}) collective-permute-start(f32[160,16]{0,1:T(8,128)S(1)} %get-tuple-element.12), channel_id=1, source_target_pairs={{0,28},{2,30},{4,0},{6,2},{8,4},{10,6},{12,8},{14,10},{16,12},{18,... | collective-permute-start | bytes 30728 | tf_op jit(solution)/shard_map/ppermute | solution.py:14
Sparse Core Ops, SparseCore 0:
  86.9 30.5 all-gather.1
  170.6 76.1 reduce-scatter.3
where the time goes:
time: 258 us; the launch traced here: 257 us
  waiting for transfers between devices  103 us (40%)
  starting transfers between devices  56.6 us (22%)
  local copies, waits for them, and re-layouts  44.8 us (17%)
  other arithmetic  31.9 us (12%)
  between operations  15.4 us (6%)
  matrix products  5.14 us (2%)
    unnamed x3, waiting for transfers between devices  76.4 us
    ppermute x32, starting transfers between devices, from_behind(): return lax.ppermute(value, axis, pairs)  56.3 us
    ppermute x32, waiting for transfers between devices, from_behind(): return lax.ppermute(value, axis, pairs)  26.6 us
    scatter-add x4, other arithmetic, operate(): summed = summed.at[:, flat_nodes].add(products.reshape(columns, -1))  24.5 us
    unnamed x21, local copies, waits for them, and re-layouts  21.9 us
    gather x4, local copies, waits for them, and re-layouts, operate(): gathered = extended[:, cell_nodes]  15.8 us
  transfers between devices with their start and end apart: 34, of which 15 were waited for; matrix products, arithmetic and copies ran while one was open for 11% of the time, Pallas kernels for 0%

commit v1 on v0

v1 whole, which is shorter than its diff:
```python
import functools
import jax
import jax.numpy as jnp
from jax import lax
from jax.experimental import pallas as pl
from jax.experimental.pallas import tpu as pltpu
from jax.sharding import PartitionSpec as P

filter_centre = 1.5
filter_half = 2.5
first_sigma = -0.625
MESH = pl.DeviceIdType.MESH
bf16 = jnp.bfloat16
f32 = jnp.float32


def sigma_values():
    values = [first_sigma]
    for _ in range(2):
        values.append(1.0 / (2.0 / first_sigma - values[-1]))
    return values


def neighbour_offset(neighbour, reach):
    if neighbour < reach:
        return neighbour + 1
    return reach - 1 - neighbour


def dot(a, b):
    return jnp.dot(a, b, preferred_element_type=f32)


def kernel(
    n, nb, width, x_ref, basis_ref, mass_ref, mats_ref, ncol_ref, nrow_ref, scol_ref, srow_ref,
    f_ref, inter_ref, ham_ref,
    full, stiff, coupled, fields, out_x, ghost, out_y, back, tile, got,
    halo_send, halo_recv, basis_send, basis_recv, local_sem, tile_send, tile_recv,
):
    me = lax.axis_index("mesh")
    mine = lax.axis_index("band")
    columns, owned = x_ref.shape
    slots = scol_ref.shape[0] // width
    reach = width // 2
    cols = basis_ref.shape[0]
    rows = full.shape[0] // n
    total = owned + width * slots

    barrier = pltpu.get_barrier_semaphore()

    def greet(d, carry):
        pl.semaphore_signal(
            barrier, inc=1, device_id=(lax.rem(me + d, n), mine), device_id_type=MESH
        )
        return carry

    lax.fori_loop(1, n, greet, 0)
    for d in range(1, nb):
        pl.semaphore_signal(
            barrier, inc=1, device_id=(me, lax.rem(mine + d, nb)), device_id_type=MESH
        )

    my_rows = pl.ds(pl.multiple_of(mine * cols, 16), cols)
    local = pltpu.make_async_copy(basis_ref, full.at[my_rows], local_sem)
    local.start()

    mass = mass_ref[...]
    send_hot = jnp.where(
        lax.broadcasted_iota(jnp.int32, (width * slots, owned), 1) == scol_ref[...], 1.0, 0.0
    ).astype(bf16)
    send_hot_t = jnp.where(
        lax.broadcasted_iota(jnp.int32, (owned, width * slots), 0) == srow_ref[...], 1.0, 0.0
    ).astype(bf16)

    pl.semaphore_wait(barrier, n - 1 + nb - 1)

    def halo(source, target, index):
        copies = []
        for k in range(width):
            partner = (k + reach) % width
            to = lax.rem(me + neighbour_offset(k, reach) + n, n)
            copies.append(
                pltpu.make_async_remote_copy(
                    src_ref=source.at[pl.ds(k * slots, slots)],
                    dst_ref=target.at[pl.ds(partner * slots, slots)],
                    send_sem=halo_send.at[index, k],
                    recv_sem=halo_recv.at[index, partner],
                    device_id=(to, mine),
                    device_id_type=MESH,
                )
            )
        return copies

    def assemble():
        corners = mats_ref.shape[1]
        for c in range(mats_ref.shape[0] // corners):
            part = pl.ds(c * corners, corners)
            hot = jnp.where(
                lax.broadcasted_iota(jnp.int32, (corners, total), 1) == ncol_ref[part, :], 1.0, 0.0
            ).astype(bf16)
            coupled[part, :] = dot(mats_ref[part, :], hot).astype(bf16)
        hot_t = jnp.where(
            lax.broadcasted_iota(jnp.int32, (total, mats_ref.shape[0]), 0) == nrow_ref[...], 1.0, 0.0
        ).astype(bf16)
        stiff[...] = dot(hot_t, coupled[...]).astype(bf16)

    started = []

    def operate(step, field):
        scaled = (mass * field.astype(f32)).astype(bf16)
        out_x[step] = dot(send_hot, scaled).astype(bf16)
        copies = halo(out_x.at[step], ghost.at[step], 2 * step)
        for copy in copies:
            copy.start()
        started.extend(copies)
        if step == 0:
            for d in range(1, nb):
                copy = pltpu.make_async_remote_copy(
                    src_ref=basis_ref,
                    dst_ref=full.at[my_rows],
                    send_sem=basis_send.at[d],
                    recv_sem=basis_recv.at[d],
                    device_id=(me, lax.rem(mine + d, nb)),
                    device_id_type=MESH,
                )
                copy.start()
            assemble()
        edge = dot(stiff[owned:, :owned], scaled)
        inner = dot(stiff[:owned, :owned], scaled)
        for copy in copies:
            copy.wait_recv()
        ghosts = ghost[step]
        out_y[step] = (edge + dot(stiff[owned:, owned:], ghosts)).astype(bf16)
        copies = halo(out_y.at[step], back.at[step], 2 * step + 1)
        for copy in copies:
            copy.start()
        started.extend(copies)
        inner = inner + dot(stiff[:owned, owned:], ghosts)
        for copy in copies:
            copy.wait_recv()
        return mass * (inner + dot(send_hot_t, back[step]))

    sigmas = sigma_values()
    previous = x_ref[...].astype(f32).T.astype(bf16)
    applied = operate(0, previous)
    current = (
        (applied - filter_centre * previous.astype(f32)) * (sigmas[0] / filter_half)
    ).astype(bf16)
    for step in range(1, 3):
        applied = operate(step, current)
        scale_now = 2.0 * sigmas[step] / filter_half
        mixing = sigmas[step - 1] * sigmas[step]
        update = (applied - filter_centre * current.astype(f32)) * scale_now - mixing * previous.astype(f32)
        previous = current
        current = update.astype(bf16)
    image = operate(3, current)
    f_ref[...] = current.astype(f32).T.astype(bf16)
    fields[...] = jnp.concatenate([current.astype(f32), image], axis=1).astype(bf16)

    local.wait()
    for d in range(1, nb):
        source = lax.rem(mine + nb - d, nb)
        its_rows = pl.ds(pl.multiple_of(source * cols, 16), cols)
        copy = pltpu.make_async_remote_copy(
            src_ref=basis_ref,
            dst_ref=full.at[its_rows],
            send_sem=basis_send.at[d],
            recv_sem=basis_recv.at[d],
            device_id=(me, lax.rem(mine + d, nb)),
            device_id_type=MESH,
        )
        copy.wait_send()
        copy.wait_recv()

    def tile_copy(d):
        return pltpu.make_async_remote_copy(
            src_ref=tile.at[d],
            dst_ref=got.at[d],
            send_sem=tile_send.at[d],
            recv_sem=tile_recv.at[d],
            device_id=(lax.rem(me + d, n), mine),
            device_id_type=MESH,
        )

    def product(target):
        return dot(full[pl.ds(pl.multiple_of(target * rows, 16), rows), :], fields[...])

    def emit(d, carry):
        tile[d] = product(lax.rem(me + d, n)).astype(bf16)
        tile_copy(d).start()
        return carry

    lax.fori_loop(1, n, emit, 0)

    def collect(d, acc):
        tile_copy(d).wait_recv()
        return acc + got[d].astype(f32)

    acc = lax.fori_loop(1, n, collect, product(me))
    inter_ref[...] = acc[:, :columns]
    ham_ref[...] = acc[:, columns:]

    for copy in started:
        copy.wait_send()

    def drain(d, carry):
        tile_copy(d).wait_send()
        return carry

    lax.fori_loop(1, n, drain, 0)


def on_device(n, nb, band_block, band_basis, mass_scale, cell_matrices, cell_nodes, cell_count, send_index):
    columns, owned = band_block.shape
    cell_slots, corners = cell_nodes.shape
    width, slots = send_index.shape[1:]
    cols = band_basis.shape[1]
    bands = cols * nb
    rows = bands // n
    count = cell_slots * corners
    total = owned + width * slots
    live = jnp.arange(cell_slots, dtype=jnp.int32)[:, None] < cell_count[0]
    nodes = jnp.where(live, cell_nodes, -1)
    vmem = pl.BlockSpec(memory_space=pltpu.VMEM)
    return pl.pallas_call(
        functools.partial(kernel, n, nb, width),
        out_shape=(
            jax.ShapeDtypeStruct((columns, owned), bf16),
            jax.ShapeDtypeStruct((rows, columns), f32),
            jax.ShapeDtypeStruct((rows, columns), f32),
        ),
        in_specs=[vmem, pl.BlockSpec(memory_space=pl.ANY)] + [vmem] * 6,
        out_specs=(vmem, vmem, vmem),
        scratch_shapes=[
            pltpu.VMEM((bands, owned), bf16),
            pltpu.VMEM((total, total), bf16),
            pltpu.VMEM((count, total), bf16),
            pltpu.VMEM((owned, 2 * columns), bf16),
            pltpu.VMEM((4, width * slots, columns), bf16),
            pltpu.VMEM((4, width * slots, columns), bf16),
            pltpu.VMEM((4, width * slots, columns), bf16),
            pltpu.VMEM((4, width * slots, columns), bf16),
            pltpu.VMEM((n, rows, 2 * columns), bf16),
            pltpu.VMEM((n, rows, 2 * columns), bf16),
            pltpu.SemaphoreType.DMA((8, width)),
            pltpu.SemaphoreType.DMA((8, width)),
            pltpu.SemaphoreType.DMA((nb,)),
            pltpu.SemaphoreType.DMA((nb,)),
            pltpu.SemaphoreType.DMA,
            pltpu.SemaphoreType.DMA((n,)),
            pltpu.SemaphoreType.DMA((n,)),
        ],
        compiler_params=pltpu.CompilerParams(collective_id=0, has_side_effects=True),
    )(
        band_block,
        band_basis.T,
        mass_scale.reshape(owned, 1),
        cell_matrices.reshape(count, corners),
        nodes.reshape(count, 1),
        nodes.reshape(1, count),
        send_index.reshape(width * slots, 1),
        send_index.reshape(1, width * slots),
    )


def solution(mesh):
    placed = (
        P("band", "mesh"),
        P("mesh", "band"),
        P("mesh"),
        P("mesh", None),
        P("mesh", None),
        P("mesh"),
        P("mesh", None, None),
    )
    return jax.shard_map(
        functools.partial(on_device, mesh.shape["mesh"], mesh.shape["band"]),
        mesh=mesh,
        in_specs=placed,
        out_specs=(P("band", "mesh"), P("mesh", "band"), P("mesh", "band")),
        check_vma=False,
    )
```

time: 258 us -> 106 us (0.41)
  the two profiles are of different devices: /device:TPU:0 before, /device:TPU:15 now
where the time goes in v1:
time: 106 us
  Pallas kernels  93.2 us (88%)
  local copies, waits for them, and re-layouts  11.4 us (11%)
  between operations  1.41 us (1%)
    pallas_call x1, Pallas kernels, on_device(): pl.pallas_call(functools.partial(kernel, n, nb, width), out_shape=(jax.Sh...  93.2 us
    pallas_call x2, local copies, waits for them, and re-layouts, on_device(): pl.pallas_call(functools.partial(kernel, n, nb, width), out_shape=(jax.Sh...  2.52 us

profile of v1, /device:TPU:15, one launch (start us, length us, event | category | flops | bytes accessed | tf_op | source)
XLA Modules:
  0.0 106.1 jit_solution(6874081905475305388)
XLA Ops:
  0.6 0.0 copy-start.4
  0.6 0.0 copy-start.2
  0.7 0.0 copy-start
  1.4 1.2 %reshape.34.srow_ref = s32[1,64]{1,0:T(1,128)} reshape(s32[1,4,16]{2,1,0:T(4,128)} %param.13) | data formatting | bytes 512 | tf_op jit(solution)/shard_map/reshape | solution.py:262
  2.6 0.0 copy-done.4
  2.6 0.1 broadcast_select_fusion
  2.7 0.7 reshape.32.nrow_ref
  3.4 1.4 %reshape.36.scol_ref = s32[64,1]{1,0:T(8,128)} reshape(s32[1,4,16]{2,1,0:T(4,128)} %param.13) | data formatting | bytes 512 | tf_op jit(solution)/shard_map/reshape | solution.py:261
  4.8 1.5 %copy.15.mass_ref = f32[256,1]{1,0:T(8,128)} copy(f32[256,1]{0,1:T(1,128)} %bitcast.5) | data formatting | bytes 2048 | tf_op jit(solution)/shard_map/reshape | solution.py:257
  6.3 0.0 copy-done.2
  6.3 1.0 reshape.30.mats_ref
  7.2 1.3 %reshape.35.ncol_ref = s32[1024,1]{1,0:T(8,128)} reshape(s32[16,64]{1,0:T(8,128)S(1)} %broadcast_select_fusion) | data formatting | bytes 8192 | tf_op jit(solution)/shard_map/reshape | solution.py:259
  8.5 0.0 copy-done
  8.5 1.2 %copy.14 = bf16[256,1536]{0,1:T(8,128)(2,1)} copy(bf16[256,1536]{1,0:T(8,128)(2,1)S(1)} %copy-done) | data formatting | bytes 1572864 | tf_op args[1]
  9.6 93.2 %shard_map.94 = (bf16[160,256]{1,0:T(8,128)(2,1)}, f32[192,160]{1,0:T(8,128)}, f32[192,160]{1,0:T(8,128)}) custom-call(bf16[160,256]{1,0:T(8,128)(2,1)} %x_ref.1, bf16[1536,256]{1,0:T(8,128)(2,1)} %bitcast.4, f32[256,1]{1,0:T(8,128)} %copy.15.mass_ref, bf16[1024,64]{1,0:T(8,128)(2,1)} %reshape.30.mats_ref, s32[1024,1]{1,0:T(8,128)} %reshape.35.ncol_ref, ...), custom_call_target="tpu_custom_call" | custom-call | tf_op jit(solution)/shard_map/pallas_call | solution.py:225
  102.8 0.0 copy-start.1
  102.8 1.7 %copy.18 = f32[192,160]{0,1:T(8,128)} copy(f32[192,160]{1,0:T(8,128)} %get-tuple-element.7) | data formatting | bytes 245760 | tf_op jit(solution)/shard_map/pallas_call | solution.py:225
  104.6 0.0 copy-done.1
  104.6 0.0 copy-start.3
  104.6 0.8 copy.19
  105.4 0.1 copy-done.3
  105.5 0.6 copy.22
  (1 shorter events, 0.0 us)
Async XLA Ops:
  0.6 2.0 %copy-start.4 = (s32[16,64]{1,0:T(8,128)S(1)}, s32[16,64]{1,0:T(8,128)}, u32[]{:S(2)}) copy-start(s32[16,64]{1,0:T(8,128)} %param.11) | copy-start | bytes 12292
  0.6 5.6 %copy-start.2 = (bf16[16,4096]{1,0:T(8,128)(2,1)S(1)}, bf16[16,4096]{1,0:T(8,128)(2,1)}, u32[]{:S(2)}) copy-start(bf16[16,4096]{1,0:T(8,128)(2,1)} %param.10) | copy-start | bytes 393220
  0.7 7.8 %copy-start = (bf16[256,1536]{1,0:T(8,128)(2,1)S(1)}, bf16[256,1536]{1,0:T(8,128)(2,1)}, u32[]{:S(2)}) copy-start(bf16[256,1536]{1,0:T(8,128)(2,1)} %param.8) | copy-start | bytes 2359300
  102.8 1.8 %copy-start.1 = (f32[192,160]{1,0:T(8,128)S(1)}, f32[192,160]{1,0:T(8,128)}, u32[]{:S(2)}) copy-start(f32[192,160]{1,0:T(8,128)} %get-tuple-element.8) | copy-start | bytes 368644
  104.6 0.9 copy-start.3

commit v2 on v1

v2 whole, which is shorter than its diff:
```python
import functools
import math
import jax
import jax.numpy as jnp
from jax import lax
from jax.experimental import pallas as pl
from jax.experimental.pallas import tpu as pltpu
from jax.sharding import PartitionSpec as P

filter_centre = 1.5
filter_half = 2.5
first_sigma = -0.625
MESH = pl.DeviceIdType.MESH
bf16 = jnp.bfloat16
f32 = jnp.float32


def sigma_values():
    values = [first_sigma]
    for _ in range(2):
        values.append(1.0 / (2.0 / first_sigma - values[-1]))
    return values


def neighbour_offset(neighbour, reach):
    if neighbour < reach:
        return neighbour + 1
    return reach - 1 - neighbour


def dot(a, b):
    return jnp.dot(a, b, preferred_element_type=f32)


def dot_nt(a, b):
    return lax.dot_general(a, b, (((1,), (1,)), ((), ())), preferred_element_type=f32)


def kernel(
    n, nb, group, packed, x_ref, basis_ref, mass_ref, mats_ref, nodes_ref, count_ref, send_ref,
    f_ref, inter_ref, ham_ref,
    full, hots, coupled, out_x, ghost, out_y, back, held, tile, got,
    halo_send, halo_recv, basis_send, basis_recv, held_send, held_recv, tile_send, tile_recv,
):
    me = lax.axis_index("mesh")
    mine = lax.axis_index("band")
    seat = lax.rem(me, group)
    team = me // group
    teams = n // group
    columns, owned = x_ref.shape
    width, slots = send_ref.shape[1:]
    reach = width // 2
    rows = full.shape[2]
    per_band = n // nb
    per_seat = per_band // group
    total = owned + width * slots
    cells, corners = nodes_ref.shape

    barrier = pltpu.get_barrier_semaphore()

    def greet(d, carry):
        pl.semaphore_signal(
            barrier, inc=1, device_id=(lax.rem(me + d, n), mine), device_id_type=MESH
        )
        return carry

    lax.fori_loop(1, n, greet, 0)
    for d in range(1, nb):
        for e in range(group):
            pl.semaphore_signal(
                barrier,
                inc=1,
                device_id=(team * group + lax.rem(seat + e, group), lax.rem(mine + d, nb)),
                device_id_type=MESH,
            )

    def basis_copy(e, d, s):
        chunk = lax.rem(seat + e, group) + group * s
        source = basis_ref.at[pl.ds(pl.multiple_of(chunk * rows, 16), rows)]
        target = full.at[seat, mine * per_seat + s]
        if e == 0 and d == 0:
            return pltpu.make_async_copy(source, target, basis_recv.at[e, d, s])
        return pltpu.make_async_remote_copy(
            src_ref=source,
            dst_ref=target,
            send_sem=basis_send.at[e, d, s],
            recv_sem=basis_recv.at[e, d, s],
            device_id=(team * group + lax.rem(seat + e, group), lax.rem(mine + d, nb)),
            device_id_type=MESH,
        )

    def basis_wait(e, d, s):
        if e == 0 and d == 0:
            basis_copy(e, d, s).wait()
            return
        copy = pltpu.make_async_remote_copy(
            src_ref=basis_ref.at[pl.ds(0, rows)],
            dst_ref=full.at[lax.rem(seat + group - e, group), lax.rem(mine + nb - d, nb) * per_seat + s],
            send_sem=basis_send.at[e, d, s],
            recv_sem=basis_recv.at[e, d, s],
            device_id=(team * group + lax.rem(seat + e, group), lax.rem(mine + d, nb)),
            device_id_type=MESH,
        )
        copy.wait_recv()

    places = [(e, d, s) for s in range(per_seat) for d in range(nb) for e in range(group)]
    away = [place for place in places if place[:2] != (0, 0)]
    for s in range(per_seat):
        basis_copy(0, 0, s).start()

    mass = jnp.broadcast_to(mass_ref[...], (8, owned)).T[:, :1]
    owned_ids = lax.broadcasted_iota(jnp.int32, (owned, slots), 0)
    hot_parts = [
        jnp.where(owned_ids == send_ref[0, k : k + 1, :], 1.0, 0.0) for k in range(width)
    ]
    send_hot_f = jnp.concatenate(hot_parts, axis=1)
    send_hot_t = send_hot_f.astype(bf16)
    send_hot = send_hot_f.T.astype(bf16)
    live = count_ref[0]
    total_ids = lax.broadcasted_iota(jnp.int32, (total, corners), 0)
    for c in range(cells):
        hot = jnp.where(
            jnp.logical_and(total_ids == nodes_ref[c : c + 1, :], c < live), 1.0, 0.0
        ).astype(bf16)
        part = slice(c * corners, (c + 1) * corners)
        hots[:, part] = hot
        coupled[:, part] = dot_nt(hot, mats_ref[part, :]).astype(bf16)

    previous = x_ref[...].astype(f32).T.astype(bf16)

    pl.semaphore_wait(barrier, n - 1 + (nb - 1) * group)

    def halo(source, target, index):
        copies = []
        for k in range(width):
            partner = (k + reach) % width
            to = lax.rem(me + neighbour_offset(k, reach) + n, n)
            copies.append(
                pltpu.make_async_remote_copy(
                    src_ref=source.at[pl.ds(k * slots, slots)],
                    dst_ref=target.at[pl.ds(partner * slots, slots)],
                    send_sem=halo_send.at[index, k],
                    recv_sem=halo_recv.at[index, partner],
                    device_id=(to, mine),
                    device_id_type=MESH,
                )
            )
        return copies

    started = []
    stiff = []
    share = -(-len(away) // 5)

    def held_copy(which, e):
        return pltpu.make_async_remote_copy(
            src_ref=held.at[which, seat],
            dst_ref=held.at[which, seat],
            send_sem=held_send.at[which, e],
            recv_sem=held_recv.at[which, e],
            device_id=(team * group + lax.rem(seat + e, group), mine),
            device_id_type=MESH,
        )

    def held_wait(which, e):
        there = lax.rem(seat + group - e, group)
        copy = pltpu.make_async_remote_copy(
            src_ref=held.at[which, seat],
            dst_ref=held.at[which, there],
            send_sem=held_send.at[which, e],
            recv_sem=held_recv.at[which, e],
            device_id=(team * group + lax.rem(seat + e, group), mine),
            device_id_type=MESH,
        )
        copy.wait_recv()

    def share_field(which):
        for e in range(1, group):
            held_copy(which, e).start()

    def product(which, place):
        value = dot_nt(held[which, 0], full[0, place])
        for i in range(1, group):
            value = value + dot_nt(held[which, i], full[i, place])
        return value

    def pack(value):
        if not packed:
            return value
        half = columns // 2
        left = rows - rows % 128
        rest = jnp.concatenate([value[:half, left:], value[half:, left:]], axis=1)
        parts = [value[:, a : a + 128] for a in range(0, left, 128)]
        return jnp.concatenate(parts + [rest], axis=0)

    def unpack(value):
        if not packed:
            return value
        half = columns // 2
        full_parts = rows // 128
        parts = [value[a * columns : (a + 1) * columns] for a in range(full_parts)]
        rest = value[full_parts * columns :]
        parts.append(jnp.concatenate([rest[:, :64], rest[:, 64:]], axis=0))
        return jnp.concatenate(parts, axis=1)

    def tile_copy(which, d):
        return pltpu.make_async_remote_copy(
            src_ref=tile.at[which, d],
            dst_ref=got.at[which, d],
            send_sem=tile_send.at[which, d],
            recv_sem=tile_recv.at[which, d],
            device_id=(lax.rem(team + d, teams) * group + seat, mine),
            device_id_type=MESH,
        )

    def tiles_out(which):
        for e in range(1, group):
            held_wait(which, e)

        def emit(d, carry):
            tile[which, d] = pack(product(which, lax.rem(team + d, teams))).astype(bf16)
            tile_copy(which, d).start()
            return carry

        lax.fori_loop(1, teams, emit, 0)

    def tiles_in(which):
        def collect(d, acc):
            tile_copy(which, d).wait_recv()
            return acc + got[which, d].astype(f32)

        return unpack(lax.fori_loop(1, teams, collect, pack(product(which, team))))

    def after_send(index):
        for place in away[share * index : share * (index + 1)]:
            basis_copy(*place).start()
        if index == 6:
            share_field(0)
        if index == 7:
            for place in places:
                basis_wait(*place)
            tiles_out(0)

    def operate(step, field):
        scaled = (mass * field.astype(f32)).astype(bf16)
        out_x[step] = dot(send_hot, scaled).astype(bf16)
        copies = halo(out_x.at[step], ghost.at[step], 2 * step)
        for copy in copies:
            copy.start()
        started.extend(copies)
        after_send(2 * step)
        if step == 0:
            stiff.append(dot_nt(hots[...], coupled[...]).astype(bf16))
        matrix = stiff[0]
        edge = dot(matrix[owned:, :owned], scaled)
        inner = dot(matrix[:owned, :owned], scaled)
        for copy in copies:
            copy.wait_recv()
        ghosts = ghost[step]
        out_y[step] = (edge + dot(matrix[owned:, owned:], ghosts)).astype(bf16)
        copies = halo(out_y.at[step], back.at[step], 2 * step + 1)
        for copy in copies:
            copy.start()
        started.extend(copies)
        after_send(2 * step + 1)
        inner = inner + dot(matrix[:owned, owned:], ghosts)
        for copy in copies:
            copy.wait_recv()
        return mass * (inner + dot(send_hot_t, back[step]))

    sigmas = sigma_values()
    applied = operate(0, previous)
    current = (
        (applied - filter_centre * previous.astype(f32)) * (sigmas[0] / filter_half)
    ).astype(bf16)
    for step in range(1, 3):
        applied = operate(step, current)
        scale_now = 2.0 * sigmas[step] / filter_half
        mixing = sigmas[step - 1] * sigmas[step]
        update = (applied - filter_centre * current.astype(f32)) * scale_now - mixing * previous.astype(f32)
        previous = current
        current = update.astype(bf16)
    turned = current.astype(f32).T.astype(bf16)
    f_ref[...] = turned
    held[0, seat] = turned
    image = operate(3, current)
    held[1, seat] = image.T.astype(bf16)
    share_field(1)
    inter_own = tiles_in(0)
    tiles_out(1)
    inter_ref[...] = inter_own
    ham_ref[...] = tiles_in(1)

    for copy in started:
        copy.wait_send()
    for place in away:
        basis_copy(*place).wait_send()
    for which in range(2):
        for e in range(1, group):
            held_copy(which, e).wait_send()

        def drain(d, carry):
            tile_copy(which, d).wait_send()
            return carry

        lax.fori_loop(1, teams, drain, 0)


def on_device(n, nb, band_block, band_basis, mass_scale, cell_matrices, cell_nodes, cell_count, send_index):
    columns, owned = band_block.shape
    cell_slots, corners = cell_nodes.shape
    width, slots = send_index.shape[1:]
    cols = band_basis.shape[1]
    rows = cols * nb // n
    count = cell_slots * corners
    total = owned + width * slots
    group = math.gcd(4, n // nb)
    teams = n // group
    packed = rows % 128 == 64 and columns % 32 == 0
    tile_shape = (columns * rows // 128, 128) if packed else (columns, rows)
    vmem = pl.BlockSpec(memory_space=pltpu.VMEM)
    smem = pl.BlockSpec(memory_space=pltpu.SMEM)
    edge_shape = pltpu.VMEM((4, width * slots, columns), bf16)
    filtered, inter, ham = pl.pallas_call(
        functools.partial(kernel, n, nb, group, packed),
        out_shape=(
            jax.ShapeDtypeStruct((columns, owned), bf16),
            jax.ShapeDtypeStruct((columns, rows), f32),
            jax.ShapeDtypeStruct((columns, rows), f32),
        ),
        in_specs=[vmem, pl.BlockSpec(memory_space=pl.ANY), vmem, vmem, vmem, smem, vmem],
        out_specs=(vmem, vmem, vmem),
        scratch_shapes=[
            pltpu.VMEM((group, teams, rows, owned), bf16),
            pltpu.VMEM((total, count), bf16),
            pltpu.VMEM((total, count), bf16),
            edge_shape,
            edge_shape,
            edge_shape,
            edge_shape,
            pltpu.VMEM((2, group, columns, owned), bf16),
            pltpu.VMEM((2, teams) + tile_shape, bf16),
            pltpu.VMEM((2, teams) + tile_shape, bf16),
            pltpu.SemaphoreType.DMA((8, width)),
            pltpu.SemaphoreType.DMA((8, width)),
            pltpu.SemaphoreType.DMA((group, nb, n // nb // group)),
            pltpu.SemaphoreType.DMA((group, nb, n // nb // group)),
            pltpu.SemaphoreType.DMA((2, group)),
            pltpu.SemaphoreType.DMA((2, group)),
            pltpu.SemaphoreType.DMA((2, teams)),
            pltpu.SemaphoreType.DMA((2, teams)),
        ],
        compiler_params=pltpu.CompilerParams(collective_id=0, has_side_effects=True),
    )(
        band_block,
        band_basis.T,
        mass_scale.reshape(1, owned),
        cell_matrices.reshape(count, corners),
        cell_nodes,
        cell_count,
        send_index,
    )
    return filtered, inter.T, ham.T


def solution(mesh):
    placed = (
        P("band", "mesh"),
        P("mesh", "band"),
        P("mesh"),
        P("mesh", None),
        P("mesh", None),
        P("mesh"),
        P("mesh", None, None),
    )
    return jax.shard_map(
        functools.partial(on_device, mesh.shape["mesh"], mesh.shape["band"]),
        mesh=mesh,
        in_specs=placed,
        out_specs=(P("band", "mesh"), P("mesh", "band"), P("mesh", "band")),
        check_vma=False,
    )
```

time: 106 us -> 61.8 us (0.58)
  the two profiles are of different devices: /device:TPU:15 before, /device:TPU:0 now
where the time goes in v2:
time: 61.8 us; the launch traced here: 61.6 us
  Pallas kernels  52.9 us (86%)
  local copies, waits for them, and re-layouts  7.4 us (12%)
  between operations  1.3 us (2%)
    pallas_call x1, Pallas kernels, on_device(): pl.pallas_call(functools.partial(kernel, n, nb, group, packed), out_shape...  52.9 us
    unnamed x8, local copies, waits for them, and re-layouts  5.51 us
    reshape x1, local copies, waits for them, and re-layouts, on_device(): cell_matrices.reshape(count, corners)  1.89 us

profile of v2, /device:TPU:0, one launch (start us, length us, event | category | flops | bytes accessed | tf_op | source)
XLA Modules:
  0.0 61.6 jit_solution(1514522093443322576)
XLA Ops:
  1.3 1.9 %reshape.13.mats_ref = bf16[1024,64]{1,0:T(8,128)(2,1)} reshape(bf16[16,4096]{1,0:T(8,128)(2,1)} %param.10) | data formatting | bytes 262144 | tf_op jit(solution)/shard_map/reshape | solution.py:357
  3.2 2.3 %copy.11 = bf16[256,1536]{0,1:T(8,128)(2,1)} copy(bf16[256,1536]{1,0:T(8,128)(2,1)} %param.8) | data formatting | bytes 1572864 | tf_op args[1]
  5.5 52.9 %shard_map.94 = (bf16[160,256]{1,0:T(8,128)(2,1)}, f32[160,192]{1,0:T(8,128)}, f32[160,192]{1,0:T(8,128)}) custom-call(bf16[160,256]{1,0:T(8,128)(2,1)} %x_ref.1, bf16[1536,256]{1,0:T(8,128)(2,1)} %bitcast.4, f32[1,256]{1,0:T(1,128)} %bitcast.7, bf16[1024,64]{1,0:T(8,128)(2,1)} %reshape.13.mats_ref, s32[16,64]{1,0:T(8,128)} %nodes_ref.1, ...), custom_call_target="tpu_custom_call" | custom-call | tf_op jit(solution)/shard_map/pallas_call | solution.py:323
  58.4 0.0 copy-start.1
  58.4 1.6 %copy.16 = bf16[160,256]{1,0:T(8,128)(2,1)} copy(bf16[160,256]{1,0:T(8,128)(2,1)} %get-tuple-element.12) | data formatting | bytes 163840
  59.9 0.0 copy-done.1
  59.9 0.0 copy-start
  59.9 0.7 %copy.17 = f32[192,160]{0,1:T(8,128)} copy(f32[192,160]{0,1:T(8,128)S(1)} %bitcast.6) | data formatting | bytes 245760
  60.6 0.3 copy-done
  60.9 0.7 %copy.18 = f32[192,160]{0,1:T(8,128)} copy(f32[192,160]{0,1:T(8,128)S(1)} %bitcast.5) | data formatting | bytes 245760
Async XLA Ops:
  58.4 1.6 %copy-start.1 = (f32[160,192]{1,0:T(8,128)S(1)}, f32[160,192]{1,0:T(8,128)}, u32[]{:S(2)}) copy-start(f32[160,192]{1,0:T(8,128)} %get-tuple-element.7) | copy-start | bytes 368644
  59.9 1.0 %copy-start = (f32[160,192]{1,0:T(8,128)S(1)}, f32[160,192]{1,0:T(8,128)}, u32[]{:S(2)}) copy-start(f32[160,192]{1,0:T(8,128)} %get-tuple-element.8) | copy-start | bytes 368644

commit v3 on v2

--- a/solution.py
+++ b/solution.py
@@ -39,8 +39,8 @@
 def kernel(
     n, nb, group, packed, x_ref, basis_ref, mass_ref, mats_ref, nodes_ref, count_ref, send_ref,
     f_ref, inter_ref, ham_ref,
-    full, hots, coupled, out_x, ghost, out_y, back, held, tile, got,
-    halo_send, halo_recv, basis_send, basis_recv, held_send, held_recv, tile_send, tile_recv,
+    full, block, turned_basis, hots, coupled, out_x, ghost, out_y, back, held, tile, got,
+    halo_send, halo_recv, block_sem, basis_send, basis_recv, held_send, held_recv, tile_send, tile_recv,
 ):
     me = lax.axis_index("mesh")
     mine = lax.axis_index("band")
@@ -76,7 +76,7 @@
 
     def basis_copy(e, d, s):
         chunk = lax.rem(seat + e, group) + group * s
-        source = basis_ref.at[pl.ds(pl.multiple_of(chunk * rows, 16), rows)]
+        source = turned_basis.at[pl.ds(pl.multiple_of(chunk * rows, 16), rows)]
         target = full.at[seat, mine * per_seat + s]
         if e == 0 and d == 0:
             return pltpu.make_async_copy(source, target, basis_recv.at[e, d, s])
@@ -94,7 +94,7 @@
             basis_copy(e, d, s).wait()
             return
         copy = pltpu.make_async_remote_copy(
-            src_ref=basis_ref.at[pl.ds(0, rows)],
+            src_ref=turned_basis.at[pl.ds(0, rows)],
             dst_ref=full.at[lax.rem(seat + group - e, group), lax.rem(mine + nb - d, nb) * per_seat + s],
             send_sem=basis_send.at[e, d, s],
             recv_sem=basis_recv.at[e, d, s],
@@ -105,8 +105,8 @@
 
     places = [(e, d, s) for s in range(per_seat) for d in range(nb) for e in range(group)]
     away = [place for place in places if place[:2] != (0, 0)]
-    for s in range(per_seat):
-        basis_copy(0, 0, s).start()
+    load = pltpu.make_async_copy(basis_ref, block, block_sem)
+    load.start()
 
     mass = jnp.broadcast_to(mass_ref[...], (8, owned)).T[:, :1]
     owned_ids = lax.broadcasted_iota(jnp.int32, (owned, slots), 0)
@@ -128,6 +128,12 @@
 
     previous = x_ref[...].astype(f32).T.astype(bf16)
 
+    load.wait()
+    for a in range(0, block.shape[1], 128):
+        turned_basis[a : a + 128, :] = block[:, a : a + 128].T
+    for s in range(per_seat):
+        basis_copy(0, 0, s).start()
+
     pl.semaphore_wait(barrier, n - 1 + (nb - 1) * group)
 
     def halo(source, target, index):
@@ -221,14 +227,14 @@
             tile_copy(which, d).start()
             return carry
 
-        lax.fori_loop(1, teams, emit, 0)
-
-    def tiles_in(which):
+        lax.fori_loop(1, teams, emit, 0, unroll=teams <= 4)
+
+    def tiles_in(which, own):
         def collect(d, acc):
             tile_copy(which, d).wait_recv()
             return acc + got[which, d].astype(f32)
 
-        return unpack(lax.fori_loop(1, teams, collect, pack(product(which, team))))
+        return unpack(lax.fori_loop(1, teams, collect, own, unroll=teams <= 4))
 
     def after_send(index):
         for place in away[share * index : share * (index + 1)]:
@@ -238,7 +244,6 @@
         if index == 7:
             for place in places:
                 basis_wait(*place)
-            tiles_out(0)
 
     def operate(step, field):
         scaled = (mass * field.astype(f32)).astype(bf16)
@@ -285,10 +290,12 @@
     image = operate(3, current)
     held[1, seat] = image.T.astype(bf16)
     share_field(1)
-    inter_own = tiles_in(0)
+    tiles_out(0)
+    inter_own = pack(product(0, team))
     tiles_out(1)
-    inter_ref[...] = inter_own
-    ham_ref[...] = tiles_in(1)
+    ham_own = pack(product(1, team))
+    inter_ref[...] = tiles_in(0, inter_own)
+    ham_ref[...] = tiles_in(1, ham_own)
 
     for copy in started:
         copy.wait_send()
@@ -331,6 +338,8 @@
         out_specs=(vmem, vmem, vmem),
         scratch_shapes=[
             pltpu.VMEM((group, teams, rows, owned), bf16),
+            pltpu.VMEM((owned, cols), bf16),
+            pltpu.VMEM((cols, owned), bf16),
             pltpu.VMEM((total, count), bf16),
             pltpu.VMEM((total, count), bf16),
             edge_shape,
@@ -342,6 +351,7 @@
             pltpu.VMEM((2, teams) + tile_shape, bf16),
             pltpu.SemaphoreType.DMA((8, width)),
             pltpu.SemaphoreType.DMA((8, width)),
+            pltpu.SemaphoreType.DMA,
             pltpu.SemaphoreType.DMA((group, nb, n // nb // group)),
             pltpu.SemaphoreType.DMA((group, nb, n // nb // group)),
             pltpu.SemaphoreType.DMA((2, group)),
@@ -352,7 +362,7 @@
         compiler_params=pltpu.CompilerParams(collective_id=0, has_side_effects=True),
     )(
         band_block,
-        band_basis.T,
+        band_basis,
         mass_scale.reshape(1, owned),
         cell_matrices.reshape(count, corners),
         cell_nodes,

time: 61.8 us -> 60.3 us (0.976)
  local copies, waits for them, and re-layouts: 7.4 us -> 5.09 us
  Pallas kernels: 52.9 us -> 53.7 us
    unnamed x8 -> x7, local copies, waits for them, and re-layouts: 5.51 us -> 3.21 us
    pallas_call x1, Pallas kernels: 52.9 us -> 53.7 us  [on_device(): pl.pallas_call(functools.partial(kernel, n, nb, group, packed), out_shape...]
where the time goes in v3:
time: 60.3 us; the launch traced here: 60.1 us
  Pallas kernels  53.7 us (89%)
  local copies, waits for them, and re-layouts  5.09 us (8%)
  between operations  1.3 us (2%)
    pallas_call x1, Pallas kernels, on_device(): pl.pallas_call(functools.partial(kernel, n, nb, group, packed), out_shape...  53.7 us
    unnamed x7, local copies, waits for them, and re-layouts  3.21 us
    reshape x1, local copies, waits for them, and re-layouts, on_device(): cell_matrices.reshape(count, corners)  1.88 us

profile of v3, /device:TPU:0, one launch (start us, length us, event | category | flops | bytes accessed | tf_op | source)
XLA Modules:
  0.0 60.1 jit_solution(9636098728200666556)
XLA Ops:
  1.3 1.9 %reshape.13.mats_ref = bf16[1024,64]{1,0:T(8,128)(2,1)} reshape(bf16[16,4096]{1,0:T(8,128)(2,1)} %param.10) | data formatting | bytes 262144 | tf_op jit(solution)/shard_map/reshape | solution.py:367
  3.2 53.7 %shard_map.94 = (bf16[160,256]{1,0:T(8,128)(2,1)}, f32[160,192]{1,0:T(8,128)}, f32[160,192]{1,0:T(8,128)}) custom-call(bf16[160,256]{1,0:T(8,128)(2,1)} %x_ref.1, bf16[256,1536]{1,0:T(8,128)(2,1)} %basis_ref.1, f32[1,256]{1,0:T(1,128)} %bitcast.5, bf16[1024,64]{1,0:T(8,128)(2,1)} %reshape.13.mats_ref, s32[16,64]{1,0:T(8,128)} %nodes_ref.1, ...), custom_call_target="tpu_custom_call" | custom-call | tf_op jit(solution)/shard_map/pallas_call | solution.py:330
  56.9 0.0 copy-start.1
  56.9 1.6 %copy.14 = bf16[160,256]{1,0:T(8,128)(2,1)} copy(bf16[160,256]{1,0:T(8,128)(2,1)} %get-tuple-element.12) | data formatting | bytes 163840
  58.5 0.0 copy-done.1
  58.5 0.0 copy-start
  58.5 0.7 %copy.15 = f32[192,160]{0,1:T(8,128)} copy(f32[192,160]{0,1:T(8,128)S(1)} %bitcast.4) | data formatting | bytes 245760
  59.1 0.3 copy-done
  59.4 0.7 %copy.16 = f32[192,160]{0,1:T(8,128)} copy(f32[192,160]{0,1:T(8,128)S(1)} %bitcast.3) | data formatting | bytes 245760
Async XLA Ops:
  56.9 1.6 %copy-start.1 = (f32[160,192]{1,0:T(8,128)S(1)}, f32[160,192]{1,0:T(8,128)}, u32[]{:S(2)}) copy-start(f32[160,192]{1,0:T(8,128)} %get-tuple-element.7) | copy-start | bytes 368644
  58.5 1.0 %copy-start = (f32[160,192]{1,0:T(8,128)S(1)}, f32[160,192]{1,0:T(8,128)}, u32[]{:S(2)}) copy-start(f32[160,192]{1,0:T(8,128)} %get-tuple-element.8) | copy-start | bytes 368644
